TPU v7x, 128 devices: a whole 4x4x4 slice. The times are simulated.
128 devices in a mesh: tok: 8 (over x, z_lo), blk: 16 (over z_hi, y, core).
Axes of the slice: x: 4, y: 4, z: 4 (z_hi: 2, z_lo: 2; z = z_hi * 2 + z_lo), core: 2. Of those that a mesh axis runs over, the one named last changes fastest.
Arguments:
- states: bfloat16 [48, 512, 1024], P('blk', 'tok'), may hold values from -6 to 6
- gain_attn: bfloat16 [1024], replicated, may hold values from 0.099609375 to 1.8984375
- w_qkv: bfloat16 [1024, 3072], replicated, may hold values from -4 to 4
- w_out: bfloat16 [1024, 1024], replicated, may hold values from -0.1875 to 0.1875
- cache_prev: bfloat16 [48, 1536, 2, 1024], P('blk', 'tok'), may hold values from -6 to 6
- cached_blocks: int32 [48], P('blk'), may hold values from 0 to 12, as said below
- gain_moe: bfloat16 [1024], replicated, may hold values from 0.099609375 to 1.8984375
- w_router: bfloat16 [1024, 16], replicated, may hold values from -0.1875 to 0.1875
- routes: int32 [8, 48, 64, 2], P('tok', 'blk'), may hold values from 0 to 15, all different within a row; in each aligned block of 192 rows (0 to 191, 192 to 383, ..., all dimensions but the last counted through in order) at most 30 rows name the same one
- w_gate_up: bfloat16 [16, 2, 1024, 2816], P('blk', None, None, 'tok'), may hold values from -0.1875 to 0.1875
- w_down: bfloat16 [16, 2816, 1024], P('blk', 'tok'), may hold values from -0.109375 to 0.109375
Outputs:
- out_hidden: bfloat16 [48, 512, 1024], P('blk', 'tok')
- decode_cache: bfloat16 [48, 2048, 2, 1024], P('blk', None, None, 'tok')
Inputs may be any that keep to these rules, and one draw needn't show every extreme that they name: `cached_blocks`: some request holds all 12 blocks. `routes`: among the 192 tokens of one device, no expert is named more than 30 times.
All inputs are finite; a program needn't handle non-finite values.
Results may differ from a plain program's by a relative error of at most 0.0065.
Values may be sent and summed in bfloat16 or wider, within the bound.
A program may use at most 192 MiB of HBM per device.

v0:
```python
import jax
import jax.numpy as jnp
from jax import lax
from jax.sharding import PartitionSpec as P

HEAD_DIM = 64
TOP = 2
BLOCK = 128


def normalize(values, gain):
    return (
        values
        * lax.rsqrt(jnp.mean(values * values, -1, keepdims=True) + 1e-06)
        * gain.astype(jnp.float32)
    )


def body(
    states,
    gain_attn,
    w_qkv,
    w_out,
    cache_prev,
    cached_blocks,
    gain_moe,
    w_router,
    routes,
    w_gate_up,
    w_down,
):
    tok_count = lax.axis_size("tok")
    blk_count = lax.axis_size("blk")
    requests, per_dev, width = states.shape
    tokens_here = requests * per_dev
    local_width = width // tok_count
    heads_here = local_width // HEAD_DIM
    cache_here = cache_prev.shape[1]
    cache_full = cache_here * tok_count
    flat_states = states.reshape(tokens_here, width).astype(jnp.float32)
    normed = normalize(flat_states, gain_attn).astype(jnp.bfloat16)
    projected = jnp.dot(normed, w_qkv, preferred_element_type=jnp.float32).astype(jnp.bfloat16)
    projected = projected.reshape(requests, per_dev, 3, tok_count, local_width)
    cache_split = cache_prev.reshape(requests, cache_here, 2, tok_count, local_width)
    heads_view, cache_heads = (
        lax.all_to_all(projected, "tok", split_axis=3, concat_axis=1, tiled=True),
        lax.all_to_all(cache_split, "tok", split_axis=3, concat_axis=1, tiled=True),
    )
    group_len = heads_view.shape[1]
    heads_view = heads_view.reshape(requests, group_len, 3, heads_here, HEAD_DIM)
    cache_heads = cache_heads.reshape(requests, cache_full, 2, heads_here, HEAD_DIM)
    lengths = cached_blocks * BLOCK
    key_all = jnp.concatenate([cache_heads[:, :, 0], heads_view[:, :, 1]], axis=1)
    value_all = jnp.concatenate([cache_heads[:, :, 1], heads_view[:, :, 2]], axis=1)
    scores = jnp.einsum(
        "rqhd,rkhd->rhqk", heads_view[:, :, 0], key_all, preferred_element_type=jnp.float32
    ) * HEAD_DIM ** (-0.5)
    key_pos = jnp.arange(cache_full + group_len)
    query_pos = jnp.arange(group_len)
    valid = jnp.where(
        key_pos[None, None, :] < cache_full,
        key_pos[None, None, :] < lengths[:, None, None],
        key_pos[None, None, :] - cache_full <= query_pos[None, :, None],
    )
    scores = jnp.where(valid[:, None], scores, -1e30)
    highest = jnp.max(scores, axis=-1, keepdims=True)
    weights = jnp.exp(scores - highest)
    weights = (weights / jnp.sum(weights, axis=-1, keepdims=True)).astype(jnp.bfloat16)
    attended = jnp.einsum(
        "rhqk,rkhd->rqhd", weights, value_all, preferred_element_type=jnp.float32
    ).astype(jnp.bfloat16)
    attended = attended.reshape(requests, tok_count, per_dev, local_width)
    gathered_back = lax.all_to_all(
        attended, "tok", split_axis=1, concat_axis=3, tiled=True
    ).reshape(tokens_here, width)
    old_part = cache_heads.reshape(requests, cache_full, 2, local_width)
    keep = jnp.arange(cache_full)[None, :, None, None] < lengths[:, None, None, None]
    base = jnp.concatenate(
        [
            jnp.where(keep, old_part, jnp.zeros((), jnp.bfloat16)),
            jnp.zeros((requests, group_len, 2, local_width), jnp.bfloat16),
        ],
        axis=1,
    )
    fresh = heads_view[:, :, 1:3].reshape(requests, group_len, 2, local_width)

    def place_one(base_one, fresh_one, length):
        return lax.dynamic_update_slice(base_one, fresh_one, (length, length * 0, length * 0))

    decode_cache = jax.vmap(place_one)(base, fresh, lengths)
    residual = flat_states + jnp.dot(gathered_back, w_out, preferred_element_type=jnp.float32)
    normed_moe = normalize(residual, gain_moe).astype(jnp.bfloat16)
    logits = jnp.dot(normed_moe, w_router, preferred_element_type=jnp.float32)
    experts_all = logits.shape[1]
    local_experts = w_gate_up.shape[0]
    route_flat = routes.reshape(tokens_here, TOP)
    chosen = jnp.sum(
        jnp.where(
            route_flat[:, :, None] == jnp.arange(experts_all)[None, None, :],
            logits[:, None, :],
            0.0,
        ),
        axis=-1,
    )
    gates = jax.nn.sigmoid(chosen)
    capacity = tokens_here * TOP * 5 // (4 * experts_all)
    assigned = route_flat.reshape(-1)
    one_hot = (assigned[:, None] == jnp.arange(experts_all)[None, :]).astype(jnp.int32)
    ranks = jnp.sum(one_hot * (jnp.cumsum(one_hot, axis=0) - 1), axis=1)
    slot_index = assigned * capacity + ranks
    placing = (jnp.arange(experts_all * capacity)[:, None] == slot_index[None, :]).astype(
        jnp.bfloat16
    )
    per_token = jnp.sum(placing.reshape(experts_all * capacity, tokens_here, TOP), axis=-1)
    outgoing = jnp.dot(per_token, normed_moe, preferred_element_type=jnp.float32).astype(
        jnp.bfloat16
    )
    outgoing = outgoing.reshape(blk_count, local_experts, capacity, width)
    incoming = lax.all_to_all(outgoing, "blk", split_axis=0, concat_axis=0, tiled=True)
    both = jnp.einsum(
        "secd,ekdf->ksecf",
        incoming,
        lax.all_gather(w_gate_up, "tok", axis=3, tiled=True),
        preferred_element_type=jnp.float32,
    )
    hidden_full = (jax.nn.gelu(both[0], approximate=True) * both[1]).astype(jnp.bfloat16)
    expert_sum = jnp.einsum(
        "secf,efd->secd",
        hidden_full,
        lax.all_gather(w_down, "tok", axis=1, tiled=True),
        preferred_element_type=jnp.float32,
    )
    expert_out = expert_sum.astype(jnp.bfloat16)
    returned = lax.all_to_all(expert_out, "blk", split_axis=0, concat_axis=0, tiled=True).reshape(
        experts_all * capacity, width
    )
    picked = jnp.dot(placing.T, returned, preferred_element_type=jnp.float32)
    mixed = jnp.sum(picked.reshape(tokens_here, TOP, width) * gates[:, :, None], axis=1)
    out_hidden = (residual + mixed).astype(jnp.bfloat16).reshape(requests, per_dev, width)
    return (out_hidden, decode_cache)


def solution(mesh):
    return jax.shard_map(
        body,
        mesh=mesh,
        in_specs=(
            P("blk", "tok", None),
            P(),
            P(),
            P(),
            P("blk", "tok", None, None),
            P("blk"),
            P(),
            P(),
            P("tok", "blk", None, None),
            P("blk", None, None, "tok"),
            P("blk", "tok", None),
        ),
        out_specs=(P("blk", "tok", None), P("blk", None, None, "tok")),
        check_vma=False,
    )
```

profile of v0, /device:TPU:1, one launch (start us, length us, event | category | flops | bytes accessed | tf_op | source)
XLA Modules:
  0.0 474.2 jit_solution(5205141952794734022)
XLA Ops:
  7.2 4.1 copy.114
  11.8 4.2 fusion.38
  16.2 1.3 copy.100
  17.6 6.2 %all-to-all-start.1 = ((bf16[3,64,3,8,128]{4,1,2,0,3:T(8,128)(2,1)}), bf16[3,64,3,8,128]{4,1,2,0,3:T(8,128)(2,1)S(1)}, u32[]{:S(2)}, u32[]{:S(2)}) async-start(bf16[3,64,3,8,128]{4,1,2,0,3:T(8,128)(2,1)} %copy.100), calls=%async_computation.1 | async-start | bytes 2359296 | tf_op jit(solution)/shard_map/all_to_all | solution.py:46
  26.0 6.4 %reshape.317 = bf16[3,192,2,8,128]{4,3,2,1,0:T(8,128)(2,1)} reshape(bf16[3,192,2,1024]{3,2,1,0:T(2,128)(2,1)} %param.15) | data formatting | bytes 4718592 | tf_op jit(solution)/shard_map/reshape | solution.py:44
  32.5 3.7 copy.96
  36.6 21.0 %all-to-all-done.1 = bf16[3,64,3,8,128]{4,1,2,0,3:T(8,128)(2,1)S(1)} async-done(((bf16[3,64,3,8,128]{4,1,2,0,3:T(8,128)(2,1)}), bf16[3,64,3,8,128]{4,1,2,0,3:T(8,128)(2,1)S(1)}, u32[]{:S(2)}, u32[]{:S(2)}) %all-to-all-start.1) | async-done | bytes 1179680 | tf_op jit(solution)/shard_map/all_to_all | solution.py:46
  57.5 7.1 %all-to-all-start = ((bf16[3,192,2,8,128]{4,1,2,0,3:T(8,128)(2,1)}), bf16[3,192,2,8,128]{4,1,2,0,3:T(8,128)(2,1)}, u32[]{:S(2)}, u32[]{:S(2)}) async-start(bf16[3,192,2,8,128]{4,1,2,0,3:T(8,128)(2,1)} %copy.96), calls=%async_computation | async-start | bytes 4718592 | tf_op jit(solution)/shard_map/all_to_all | solution.py:47
  65.4 3.5 broadcast_select_fusion.1
  70.7 1.0 eq.75
  71.8 2.6 copy.101
  74.4 3.4 reshape.266
  77.9 1.1 slice_bitcast_fusion.2
  78.9 24.0 %all-to-all-done = bf16[3,192,2,8,128]{4,1,2,0,3:T(8,128)(2,1)} async-done(((bf16[3,192,2,8,128]{4,1,2,0,3:T(8,128)(2,1)}), bf16[3,192,2,8,128]{4,1,2,0,3:T(8,128)(2,1)}, u32[]{:S(2)}, u32[]{:S(2)}) %all-to-all-start) | async-done | bytes 2359328 | tf_op jit(solution)/shard_map/all_to_all | solution.py:47
  103.0 3.3 copy.147
  106.3 9.1 %reshape.319 = bf16[3,1536,2,2,64]{4,3,1,2,0:T(2,128)(2,1)} reshape(bf16[3,8,192,2,1,128]{5,2,1,3,0,4:T(8,128)(2,1)} %bitcast.160) | data formatting | bytes 4718592 | tf_op jit(solution)/shard_map/reshape | solution.py:51
  115.4 7.2 %fusion.76 = (bf16[3,1536,1,2,64]{4,3,1,2,0:T(2,128)(2,1)}, bf16[3,1536,1,2,64]{4,3,1,2,0:T(2,128)(2,1)}) fusion(bf16[3,1536,2,2,64]{4,3,1,2,0:T(2,128)(2,1)} %reshape.319), kind=kLoop, calls=%fused_computation.105 | loop fusion | bytes 4718592 | tf_op jit(solution)/shard_map/slice | solution.py:54
  122.5 6.5 %copy.130 = bf16[3,1536,1,2,64]{1,4,3,0,2:T(8,128)(2,1)} copy(bf16[3,1536,1,2,64]{4,3,1,2,0:T(2,128)(2,1)} %get-tuple-element.43) | data formatting | bytes 2359296
  129.0 6.5 %copy.127 = bf16[3,1536,1,2,64]{1,4,3,0,2:T(8,128)(2,1)} copy(bf16[3,1536,1,2,64]{4,3,1,2,0:T(2,128)(2,1)} %get-tuple-element.42) | data formatting | bytes 2359296
  135.5 15.2 %fusion.78 = (f32[3,2,512]{2,1,0:T(2,128)S(1)}, f32[3,2,512,2048]{3,2,1,0:T(8,128)}) fusion(pred[3,512,2048]{2,1,0:T(8,128)(4,1)} %broadcast_select_fusion.1, bf16[3,512,2,64]{1,3,2,0:T(8,128)(2,1)} %get-tuple-element.47, bf16[3,1536,2,64]{1,3,2,0:T(8,128)(2,1)} %bitcast.169, bf16[3,512,3,2,64]{1,4,3,2,0:T(8,128)(2,1)S(1)} %reshape.266), kind=kOutput, calls=%fused_computation.107 | convolution fusion | flops 833619968 | bytes 30289920 | tf_op jit(solution)/shard_map/sub | solution.py:67
  150.7 11.9 %fusion.47 = bf16[3,512,2,64]{1,3,2,0:T(8,128)(2,1)} fusion(f32[3,2,512,2048]{3,2,1,0:T(8,128)} %get-tuple-element.51, f32[3,2,512]{2,1,0:T(2,128)S(1)} %get-tuple-element.50, bf16[3,512,2,64]{1,3,2,0:T(8,128)(2,1)} %get-tuple-element.46, bf16[3,1536,2,64]{1,3,2,0:T(8,128)(2,1)} %bitcast.168), kind=kOutput, calls=%fused_computation.49 | convolution fusion | flops 821231616 | bytes 27144192 | tf_op jit(solution)/shard_map/rhqk,rkhd->rqhd/dot_general | solution.py:69
  162.5 1.6 reshape.267
  164.1 1.2 copy.106
  165.4 9.9 %all-to-all-start.2 = ((bf16[3,8,64,128]{3,2,0,1:T(8,128)(2,1)}), bf16[3,8,64,128]{3,2,0,1:T(8,128)(2,1)S(1)}, u32[]{:S(2)}, u32[]{:S(2)}) async-start(bf16[3,8,64,128]{3,2,0,1:T(8,128)(2,1)} %copy.106), calls=%async_computation.2 | async-start | bytes 786432 | tf_op jit(solution)/shard_map/all_to_all | solution.py:73
  175.4 9.1 %all-to-all-done.2 = bf16[3,8,64,128]{3,2,0,1:T(8,128)(2,1)S(1)} async-done(((bf16[3,8,64,128]{3,2,0,1:T(8,128)(2,1)}), bf16[3,8,64,128]{3,2,0,1:T(8,128)(2,1)S(1)}, u32[]{:S(2)}, u32[]{:S(2)}) %all-to-all-start.2) | async-done | bytes 393248 | tf_op jit(solution)/shard_map/all_to_all | solution.py:73
  185.6 1.5 convolution_convert_fusion.1
  187.0 2.3 reshape.270
  189.3 10.3 %all-to-all-start.3 = ((bf16[16,1,30,1024]{3,2,1,0:T(8,128)(2,1)}), bf16[16,1,30,1024]{3,2,1,0:T(8,128)(2,1)}, u32[]{:S(2)}, u32[]{:S(2)}) async-start(bf16[16,1,30,1024]{3,2,1,0:T(8,128)(2,1)} %bitcast.164), calls=%async_computation.3 | async-start | bytes 2097152 | tf_op jit(solution)/shard_map/all_to_all | solution.py:119
  199.7 2.1 slice.70
  201.9 2.9 bitcast_select_fusion
  204.7 22.5 %copy.132 = bf16[3,1536,2,128]{3,2,1,0:T(2,128)(2,1)S(1)} copy(bf16[3,1536,2,128]{3,1,2,0:T(8,128)(2,1)S(1)} %bitcast_select_fusion) | data formatting | bytes 4718592
  227.2 9.2 %concatenate.14.clone = bf16[3,2048,2,128]{3,2,1,0:T(2,128)(2,1)} pad(bf16[3,1536,2,128]{3,2,1,0:T(2,128)(2,1)S(1)} %copy.132, bf16[]{:T(256)} %constant.15.clone.1), padding=0_0x0_512x0_0x0_0 | pad | bytes 5505026 | tf_op jit(solution)/shard_map/concatenate | solution.py:78
  236.4 58.9 %all-gather.3.cloned.1.call-done = bf16[1,2,1024,2816]{2,1,0,3:T(2,128)(2,1)} async-done(((bf16[1,2,1024,352]{2,1,0,3:T(2,128)(2,1)}), bf16[1,2,1024,2816]{2,1,0,3:T(2,128)(2,1)}) %all-gather.3.cloned.1.call-update) | async-done | bytes 11534352 | tf_op jit(solution)/shard_map/all_gather | solution.py:123
  295.3 28.8 %copy.115 = bf16[1,2,1024,2816]{3,2,1,0:T(8,128)(2,1)} copy(bf16[1,2,1024,2816]{2,1,0,3:T(2,128)(2,1)} %all-gather.3.cloned.1.call-done) | data formatting | bytes 23068672 | tf_op jit(solution)/shard_map/all_gather | solution.py:123
  324.0 11.8 %fusion.9 = f32[2,16,1,30,2816]{4,3,0,1,2:T(8,128)} fusion(bf16[1,2,1024,2816]{3,2,1,0:T(8,128)(2,1)} %copy.115, bf16[16,1,30,1024]{3,2,1,0:T(8,128)(2,1)} %all-to-all-done.3), kind=kOutput, calls=%fused_computation.17 | convolution fusion | flops 5536481280 | bytes 23330816 | tf_op jit(solution)/shard_map/secd,ekdf->ksecf/dot_general | solution.py:120
  335.8 81.3 %all-gather.5.cloned.1.call-done = bf16[1,2816,1024]{2,1,0:T(8,128)(2,1)} async-done(((bf16[1,352,1024]{2,1,0:T(8,128)(2,1)}), bf16[1,2816,1024]{2,1,0:T(8,128)(2,1)}) %all-gather.5.cloned.1.call-update) | async-done | bytes 5767184 | tf_op jit(solution)/shard_map/all_gather | solution.py:130
  417.1 10.8 %fusion.39 = bf16[16,1,30,1024]{3,2,1,0:T(8,128)(2,1)} fusion(bf16[1,2816,1024]{2,1,0:T(8,128)(2,1)} %all-gather.5.cloned.1.call-done, f32[2,16,1,30,2816]{4,3,0,1,2:T(8,128)} %fusion.9), kind=kOutput, calls=%fused_computation.46 | convolution fusion | flops 2782248960 | bytes 17563648 | tf_op jit(solution)/shard_map/secf,efd->secd/dot_general | solution.py:127
  427.9 7.5 %all-to-all-start.4 = ((bf16[16,1,30,1024]{3,2,1,0:T(8,128)(2,1)}), bf16[16,1,30,1024]{3,2,1,0:T(8,128)(2,1)}, u32[]{:S(2)}, u32[]{:S(2)}) async-start(bf16[16,1,30,1024]{3,2,1,0:T(8,128)(2,1)} %fusion.39), calls=%async_computation.4 | async-start | bytes 2097152 | tf_op jit(solution)/shard_map/all_to_all | solution.py:134
  435.4 26.5 %while.1 = (s32[]{:T(128)}, bf16[3,2048,2,128]{3,2,1,0:T(2,128)(2,1)}, s32[3,4]{1,0:T(4,128)S(1)}, bf16[3,512,2,128]{1,3,2,0:T(8,128)(2,1)}, s32[]{:T(128)}, /*index=5*/s32[4]{0:T(128)S(1)}) while((s32[]{:T(128)}, bf16[3,2048,2,128]{3,2,1,0:T(2,128)(2,1)}, s32[3,4]{1,0:T(4,128)S(1)}, bf16[3,512,2,128]{1,3,2,0:T(8,128)(2,1)}, s32[]{:T(128)}, ...), condition=%wide.while_cond, body=%wide.while_body.sunk | while | flops 131101 | bytes 1836718 | solution.py:88
  436.0 3.2 and_reduce_fusion.2
  440.4 3.8 fusion.88
  444.9 3.2 and_reduce_fusion.2
  449.3 3.8 fusion.88
  453.7 3.2 and_reduce_fusion.2
  457.0 1.0 constant_dynamic-slice_fusion.5
  458.1 3.8 fusion.88
  462.2 2.3 reshape.316
  464.5 2.0 multiply_reduce_fusion
  (79 shorter events, 12.7 us)
Async XLA Ops:
  7.2 177.7 %copy-start = (bf16[1024,1024]{1,0:T(8,128)(2,1)S(1)}, bf16[1024,1024]{1,0:T(8,128)(2,1)}, u32[]{:S(2)}) copy-start(bf16[1024,1024]{1,0:T(8,128)(2,1)} %param.14) | copy-start | bytes 6291460
  7.2 4.2 copy-start.2
  7.2 4.4 copy-start.7
  7.2 288.1 %all-gather.3.cloned.1.call-start = ((), (), s32[]{:S(2)}) async-start(), calls=%async_computation.5 | async-start | bytes 12976128 | tf_op jit(solution)/shard_map/all_gather | solution.py:123
  16.2 8.3 %copy-start.6 = (s32[1,3,64,2]{2,3,1,0:T(2,128)S(1)}, s32[1,3,64,2]{2,3,1,0:T(2,128)}, u32[]{:S(2)}) copy-start(s32[1,3,64,2]{2,3,1,0:T(2,128)} %param.19) | copy-start | bytes 4612
  17.6 40.0 %all-to-all-start.1 = ((bf16[3,64,3,8,128]{4,1,2,0,3:T(8,128)(2,1)}), bf16[3,64,3,8,128]{4,1,2,0,3:T(8,128)(2,1)S(1)}, u32[]{:S(2)}, u32[]{:S(2)}) async-start(bf16[3,64,3,8,128]{4,1,2,0,3:T(8,128)(2,1)} %copy.100), calls=%async_computation.1 | async-start | bytes 2359296 | tf_op jit(solution)/shard_map/all_to_all | solution.py:46
  23.8 393.4 %all-gather.5.cloned.1.call-start = ((), (), s32[]{:S(2)}) async-start(), calls=%async_computation.6 | async-start | bytes 6488064 | tf_op jit(solution)/shard_map/all_gather | solution.py:130
  32.5 3.8 copy-start.10
  32.5 3.8 copy-start.9
  57.5 45.4 %all-to-all-start = ((bf16[3,192,2,8,128]{4,1,2,0,3:T(8,128)(2,1)}), bf16[3,192,2,8,128]{4,1,2,0,3:T(8,128)(2,1)}, u32[]{:S(2)}, u32[]{:S(2)}) async-start(bf16[3,192,2,8,128]{4,1,2,0,3:T(8,128)(2,1)} %copy.96), calls=%async_computation | async-start | bytes 4718592 | tf_op jit(solution)/shard_map/all_to_all | solution.py:47
  64.6 6.0 %copy-start.8 = (bf16[1024]{0:T(1024)(128)(2,1)S(1)}, bf16[1024]{0:T(1024)(128)(2,1)}, u32[]{:S(2)}) copy-start(bf16[1024]{0:T(1024)(128)(2,1)} %param.17) | copy-start | bytes 6148
  77.8 57.6 %copy-start.1 = (bf16[3,512,3,2,64]{1,4,3,2,0:T(8,128)(2,1)}, bf16[3,512,3,2,64]{1,4,3,2,0:T(8,128)(2,1)S(1)}, u32[]{:S(2)}) copy-start(bf16[3,512,3,2,64]{1,4,3,2,0:T(8,128)(2,1)S(1)} %reshape.266) | copy-start | bytes 3538948
  162.5 22.3 %copy-start.3 = (bf16[3,64,1024]{2,1,0:T(8,128)(2,1)S(1)}, bf16[3,64,1024]{2,1,0:T(8,128)(2,1)}, u32[]{:S(2)}) copy-start(bf16[3,64,1024]{2,1,0:T(8,128)(2,1)} %param.11) | copy-start | bytes 1179652
  165.4 19.2 %all-to-all-start.2 = ((bf16[3,8,64,128]{3,2,0,1:T(8,128)(2,1)}), bf16[3,8,64,128]{3,2,0,1:T(8,128)(2,1)S(1)}, u32[]{:S(2)}, u32[]{:S(2)}) async-start(bf16[3,8,64,128]{3,2,0,1:T(8,128)(2,1)} %copy.106), calls=%async_computation.2 | async-start | bytes 786432 | tf_op jit(solution)/shard_map/all_to_all | solution.py:73
  189.3 134.7 %all-to-all-start.3 = ((bf16[16,1,30,1024]{3,2,1,0:T(8,128)(2,1)}), bf16[16,1,30,1024]{3,2,1,0:T(8,128)(2,1)}, u32[]{:S(2)}, u32[]{:S(2)}) async-start(bf16[16,1,30,1024]{3,2,1,0:T(8,128)(2,1)} %bitcast.164), calls=%async_computation.3 | async-start | bytes 2097152 | tf_op jit(solution)/shard_map/all_to_all | solution.py:119
  335.8 99.5 %copy-start.5 = (s32[4]{0:T(128)S(1)}, s32[4]{0:T(128)}, u32[]{:S(2)}) copy-start(s32[4]{0:T(128)} %constant.162) | copy-start | bytes 52
  427.9 34.3 %all-to-all-start.4 = ((bf16[16,1,30,1024]{3,2,1,0:T(8,128)(2,1)}), bf16[16,1,30,1024]{3,2,1,0:T(8,128)(2,1)}, u32[]{:S(2)}, u32[]{:S(2)}) async-start(bf16[16,1,30,1024]{3,2,1,0:T(8,128)(2,1)} %fusion.39), calls=%async_computation.4 | async-start | bytes 2097152 | tf_op jit(solution)/shard_map/all_to_all | solution.py:134
  435.4 26.5 %copy-start.4 = (bf16[1024,16]{0,1:T(8,128)(2,1)S(1)}, bf16[1024,16]{0,1:T(8,128)(2,1)}, u32[]{:S(2)}) copy-start(bf16[1024,16]{0,1:T(8,128)(2,1)} %param.18) | copy-start | bytes 98308
Sparse Core Ops, SparseCore 0:
  11.5 283.7 all-gather.2
  296.9 120.1 all-gather.4
where the time goes:
time: 477 us; the launch traced here: 474 us
  waiting for transfers between devices  195 us (41%)
  local copies, waits for them, and re-layouts  135 us (28%)
  matrix products  58.2 us (12%)
  starting transfers between devices  41.1 us (9%)
  other arithmetic  30.9 us (6%)
  between operations  14.3 us (3%)
    all_gather x1, waiting for transfers between devices, body(): lax.all_gather(w_down, 'tok', axis=1, tiled=True)  81.3 us
    all_gather x1, waiting for transfers between devices, body(): lax.all_gather(w_gate_up, 'tok', axis=3, tiled=True)  58.9 us
    unnamed x31, local copies, waits for them, and re-layouts  40.1 us
    all_gather x1, local copies, waits for them, and re-layouts, body(): lax.all_gather(w_gate_up, 'tok', axis=3, tiled=True)  28.8 us
    all_to_all x1, waiting for transfers between devices, body(): lax.all_to_all(cache_split, 'tok', split_axis=3, concat_axis=1, tiled=True)  24 us
    scatter x6, other arithmetic  21.1 us
    all_to_all x1, waiting for transfers between devices, body(): lax.all_to_all(projected, 'tok', split_axis=3, concat_axis=1, tiled=True)  21 us
    sub x1, matrix products, body(): weights = jnp.exp(scores - highest)  15.2 us
  transfers between devices with their start and end apart: 7, of which 5 were waited for; matrix products, arithmetic and copies ran while one was open for 43% of the time, Pallas kernels for 0%

commit v1 on v0

v1 whole, which is shorter than its diff:
```python
import jax
import jax.numpy as jnp
from jax import lax
from jax.experimental import pallas as pl
from jax.experimental.pallas import tpu as pltpu
from jax.sharding import PartitionSpec as P

MESH = pl.DeviceIdType.MESH
F32, BF16 = jnp.float32, jnp.bfloat16
NT = (((1,), (1,)), ((), ()))
TN = (((0,), (0,)), ((), ()))
REQ, PER, D = 3, 64, 1024
TOK = REQ * PER
N_TOK, N_BLK, N_X = 8, 16, 4
PEERS = 2 * N_BLK
SLOTS = 32
CACHE, NEW = 1536, 512
PART = CACHE // N_TOK
FFS = 352
QROWS = 256
CHUNK = 256
LANES = 128


def normed_of(values, gain):
    return values * lax.rsqrt(jnp.mean(values * values, -1, keepdims=True) + 1e-06) * gain


def layer_kernel(
    blocks,
    states,
    gains,
    routes,
    router,
    w_qkv,
    w_out,
    cache,
    w_gu,
    w_dn,
    out,
    cache_out,
    kv_out,
    wqkv,
    wout,
    cbuf,
    qs,
    qr,
    kbuf,
    vbuf,
    wide,
    asend,
    arecv,
    resid,
    place0,
    place1,
    dsend,
    drecv,
    wg,
    wd,
    acc,
    rsend,
    rrecv,
    local,
    cache_s,
    cache_r,
    cache_l,
    qkv_s,
    qkv_r,
    att_s,
    att_r,
    att_l,
    own_s,
    own_r,
    fwd_s,
    fwd_r,
    disp_s,
    disp_r,
    ret_s,
    ret_r,
):
    me = lax.axis_index("tok")
    mb = lax.axis_index("blk")
    mx, mz = me // 2, me % 2
    mine = mz * N_BLK + mb
    right = ((mx + 1) % N_X) * 2 + mz
    left = ((mx + N_X - 1) % N_X) * 2 + mz

    def remote(src, dst, ssem, rsem, **where):
        return pltpu.make_async_remote_copy(
            src_ref=src,
            dst_ref=dst,
            send_sem=ssem,
            recv_sem=rsem,
            device_id=where,
            device_id_type=MESH,
        )

    def lanes(t):
        return pl.ds(pl.multiple_of(t * LANES, LANES), LANES)

    barrier = pltpu.get_barrier_semaphore()
    for d in range(1, N_TOK):
        pl.semaphore_signal(
            barrier, inc=1, device_id={"tok": (me + d) % N_TOK}, device_id_type=MESH
        )

    def greet(d, carry):
        j = (mine + d) % PEERS
        pl.semaphore_signal(
            barrier,
            inc=1,
            device_id={"tok": mx * 2 + j // N_BLK, "blk": j % N_BLK},
            device_id_type=MESH,
        )
        return carry

    lax.fori_loop(1, PEERS, greet, 0)

    load_qkv = pltpu.make_async_copy(w_qkv, wqkv, local.at[0])
    load_out = pltpu.make_async_copy(w_out, wout, local.at[1])
    load_gu = pltpu.make_async_copy(w_gu, wg.at[0], local.at[2])
    load_dn = pltpu.make_async_copy(w_dn, wd.at[0], local.at[3])
    load_qkv.start()
    pl.semaphore_wait(barrier, N_TOK - 1 + PEERS - 1)

    def cache_copy(r, d):
        t = (me + d) % N_TOK
        return remote(
            cache.at[r, :, :, lanes(t)],
            cbuf.at[r, me],
            cache_s.at[r, d],
            cache_r.at[r, d],
            tok=t,
        )

    def cache_own(r):
        return pltpu.make_async_copy(cache.at[r, :, :, lanes(me)], cbuf.at[r, me], cache_l.at[r])

    def send_cache(r):
        cache_own(r).start()
        for d in range(1, N_TOK):
            cache_copy(r, d).start()

    send_cache(0)
    load_out.start()
    load_gu.start()
    load_dn.start()

    with jax.named_scope("project"):
        flat = states[...].astype(F32)
        normed = normed_of(flat, gains[0:1, :]).astype(BF16)
        load_qkv.wait()
        for c in range(12):
            part = jnp.dot(
                normed, wqkv[:, c * 256 : (c + 1) * 256], preferred_element_type=F32
            ).astype(BF16)
            j, t = c // 4, (c % 4) * 2
            for half in range(2):
                qs[t + half, j * REQ : (j + 1) * REQ] = part[
                    :, half * LANES : (half + 1) * LANES
                ].reshape(REQ, PER, LANES)

    def qkv_copy(d):
        t = (me + d) % N_TOK
        return remote(qs.at[t], qr.at[:, me], qkv_s.at[d], qkv_r.at[d], tok=t)

    qkv_own = pltpu.make_async_copy(qs.at[me], qr.at[:, me], local.at[4])
    qkv_own.start()
    for d in range(1, N_TOK):
        qkv_copy(d).start()
    send_cache(1)
    send_cache(2)

    def chunk_of(ref_g, ref_d, c, lo, rows):
        if c < 2:
            return ref_g.at[pl.ds(c * FFS + lo, rows)]
        return ref_d.at[pl.ds(lo, rows)]

    def own_copy(c, side):
        return remote(
            chunk_of(w_gu, w_dn, c, 0, FFS),
            chunk_of(wg.at[1 + side], wd.at[1 + side], c, 0, FFS),
            own_s.at[c, side],
            own_r.at[c, side],
            tok=right if side == 0 else left,
        )

    def fwd_copy(c, side):
        lo = side * (FFS // 2)
        return remote(
            chunk_of(wg.at[1 + side], wd.at[1 + side], c, lo, FFS // 2),
            chunk_of(wg.at[3], wd.at[3], c, lo, FFS // 2),
            fwd_s.at[c, side],
            fwd_r.at[c, side],
            tok=right if side == 0 else left,
        )

    def send_own(c):
        for side in range(2):
            own_copy(c, side).start()

    def forward(c):
        for side in range(2):
            own_copy(c, side).wait_recv()
            fwd_copy(c, side).start()

    send_own(0)

    with jax.named_scope("places"):
        r0, r1 = routes[0:1, :], routes[1:2, :]
        expert = lax.broadcasted_iota(jnp.int32, (N_BLK, TOK), 0)
        hot0 = (expert == r0).astype(F32)
        hot1 = (expert == r1).astype(F32)
        earlier = (
            lax.broadcasted_iota(jnp.int32, (TOK, TOK), 0)
            < lax.broadcasted_iota(jnp.int32, (TOK, TOK), 1)
        ).astype(BF16)
        before0 = jnp.dot(hot0.astype(BF16), earlier, preferred_element_type=F32)
        before1 = jnp.dot(hot1.astype(BF16), earlier, preferred_element_type=F32)
        before1 = before1 + jnp.sum(hot0, axis=1, keepdims=True)
        rank0 = jnp.sum(before0 * hot0, axis=0, keepdims=True).astype(jnp.int32)
        rank1 = jnp.sum(before1 * hot1, axis=0, keepdims=True).astype(jnp.int32)
        slot = lax.broadcasted_iota(jnp.int32, (N_BLK * SLOTS, TOK), 0)
        place0[...] = (slot == r0 * SLOTS + rank0).astype(F32).astype(BF16)
        place1[...] = (slot == r1 * SLOTS + rank1).astype(F32).astype(BF16)

    qkv_own.wait()
    for d in range(1, N_TOK):
        s = (me + N_TOK - d) % N_TOK
        remote(qs.at[s], qr.at[:, s], qkv_s.at[d], qkv_r.at[d], tok=s).wait_recv()

    low_head = lax.broadcasted_iota(jnp.int32, (QROWS, LANES), 1) < LANES // 2

    def att_copy(r, d):
        t = (me + d) % N_TOK
        return remote(
            asend.at[t, r],
            arecv.at[pl.ds(pl.multiple_of(r * PER, PER), PER), lanes(me)],
            att_s.at[r, d],
            att_r.at[r, d],
            tok=t,
        )

    def att_own(r):
        return pltpu.make_async_copy(
            asend.at[me, r],
            arecv.at[pl.ds(pl.multiple_of(r * PER, PER), PER), lanes(me)],
            att_l.at[r],
        )

    def one_request(r, carry):
        cache_own(r).wait()
        for d in range(1, N_TOK):
            s = (me + N_TOK - d) % N_TOK
            remote(
                cache.at[r, :, :, lanes(s)], cbuf.at[r, s], cache_s.at[r, d], cache_r.at[r, d], tok=s
            ).wait_recv()

        def split(s, inner):
            wide[...] = cbuf.at[r, s].reshape(2 * PART, LANES)[...].astype(F32)
            rows = pl.ds(pl.multiple_of(s * PART, PART), PART)
            kbuf[rows, :] = wide[pl.ds(0, PART, stride=2), :].astype(BF16)
            vbuf[rows, :] = wide[pl.ds(1, PART, stride=2), :].astype(BF16)
            return inner

        lax.fori_loop(0, N_TOK, split, 0)
        kbuf[CACHE:, :] = qr[REQ + r].reshape(NEW, LANES)
        vbuf[CACHE:, :] = qr[2 * REQ + r].reshape(NEW, LANES)
        length = blocks[r] * LANES
        old_bias = jnp.where(
            lax.broadcasted_iota(jnp.int32, (1, CACHE), 1) < length, 0.0, -1e30
        )
        for b in range(NEW // QROWS):
            keys = (b + 1) * QROWS
            query = qr[r, b * 4 : (b + 1) * 4].reshape(QROWS, LANES).astype(F32) * 0.125
            new_bias = jnp.where(
                lax.broadcasted_iota(jnp.int32, (QROWS, keys), 1)
                <= lax.broadcasted_iota(jnp.int32, (QROWS, keys), 0) + b * QROWS,
                0.0,
                -1e30,
            )
            heads = []
            for h in range(2):
                own = low_head if h == 0 else jnp.logical_not(low_head)
                one = jnp.where(own, query, 0.0).astype(BF16)
                old = (
                    lax.dot_general(one, kbuf[:CACHE, :], NT, preferred_element_type=F32)
                    + old_bias
                )
                new = (
                    lax.dot_general(
                        one, kbuf[CACHE : CACHE + keys, :], NT, preferred_element_type=F32
                    )
                    + new_bias
                )
                top = jnp.maximum(
                    jnp.max(old, axis=1, keepdims=True), jnp.max(new, axis=1, keepdims=True)
                )
                old = jnp.exp(old - top)
                new = jnp.exp(new - top)
                total = jnp.sum(old, axis=1, keepdims=True) + jnp.sum(new, axis=1, keepdims=True)
                value = jnp.dot(
                    old.astype(BF16), vbuf[:CACHE, :], preferred_element_type=F32
                ) + jnp.dot(
                    new.astype(BF16), vbuf[CACHE : CACHE + keys, :], preferred_element_type=F32
                )
                heads.append(value / total)
            both = jnp.where(low_head, heads[0], heads[1]).astype(BF16)
            asend[b * 4 : (b + 1) * 4, r] = both.reshape(4, PER, LANES)
        att_own(r).start()
        for d in range(1, N_TOK):
            att_copy(r, d).start()
        return carry

    with jax.named_scope("attend"):
        lax.fori_loop(0, REQ, one_request, 0)

    send_own(1)
    send_own(2)
    keep_cache = pltpu.make_async_copy(cbuf, cache_out, local.at[5])
    keep_cache.start()

    for r in range(REQ):
        att_own(r).wait()
        for d in range(1, N_TOK):
            s = (me + N_TOK - d) % N_TOK
            remote(
                asend.at[s, r],
                arecv.at[pl.ds(r * PER, PER), lanes(s)],
                att_s.at[r, d],
                att_r.at[r, d],
                tok=s,
            ).wait_recv()

    with jax.named_scope("dispatch"):
        load_out.wait()
        resid[...] = states[...].astype(F32) + jnp.dot(
            arecv[...], wout[...], preferred_element_type=F32
        )
        moe_in = normed_of(resid[...], gains[1:2, :]).astype(BF16)
        both_places = (place0[...].astype(F32) + place1[...].astype(F32)).astype(BF16)
        dsend[...] = (
            jnp.dot(both_places, moe_in, preferred_element_type=F32)
            .astype(BF16)
            .reshape(N_BLK, SLOTS, D)
        )

    def disp_copy(d):
        j = (mine + d) % PEERS
        e = j % N_BLK
        return remote(
            dsend.at[e],
            drecv.at[mine],
            disp_s.at[d],
            disp_r.at[d],
            tok=mx * 2 + j // N_BLK,
            blk=e,
        )

    disp_own = pltpu.make_async_copy(dsend.at[mb], drecv.at[mine], local.at[6])
    disp_own.start()

    def start_disp(d, carry):
        disp_copy(d).start()
        return carry

    lax.fori_loop(1, PEERS, start_disp, 0)
    forward(0)

    with jax.named_scope("gates"):
        logits = lax.dot_general(router[...], moe_in, NT, preferred_element_type=F32)
        diag = lax.broadcasted_iota(jnp.int32, (TOK, TOK), 0) == lax.broadcasted_iota(
            jnp.int32, (TOK, TOK), 1
        )
        gate_cols = []
        for hot in (hot0, hot1):
            chosen = jnp.sum(jnp.where(hot > 0.5, logits, 0.0), axis=0, keepdims=True)
            gate = jax.nn.sigmoid(chosen)
            gate_cols.append(jnp.sum(jnp.where(diag, gate, 0.0), axis=1, keepdims=True))

    with jax.named_scope("fresh"):

        def pair(i, carry):
            r, s = i // 4, (i % 4) * 2
            for which in range(2):
                piece = qr[(1 + which) * REQ + r, pl.ds(s, 2)].reshape(2 * PER, LANES)
                wide[pl.ds(which, 2 * PER, stride=2), :] = piece.astype(F32)
            kv_out[pl.ds(pl.multiple_of(i * 256, 256), 256), :] = wide[:256, :].astype(BF16)
            return carry

        lax.fori_loop(0, REQ * 4, pair, 0)

    disp_own.wait()

    def wait_disp(d, carry):
        j = (mine + PEERS - d) % PEERS
        remote(
            dsend.at[j % N_BLK], drecv.at[j], disp_s.at[d], disp_r.at[d], tok=mx * 2 + 1 - mz
        ).wait_recv()
        return carry

    lax.fori_loop(1, PEERS, wait_disp, 0)

    def expert(k, i):
        first = pl.multiple_of(i * (CHUNK // SLOTS), CHUNK // SLOTS)
        rows = drecv[pl.ds(first, CHUNK // SLOTS)].reshape(CHUNK, D)
        gate = lax.dot_general(rows, wg[k, :FFS, :], NT, preferred_element_type=F32)
        up = lax.dot_general(rows, wg[k, FFS:, :], NT, preferred_element_type=F32)
        hidden = (jax.nn.gelu(gate, approximate=True) * up).astype(BF16)
        return first, jnp.dot(hidden, wd[k], preferred_element_type=F32)

    def arow(i):
        return pl.ds(pl.multiple_of(i * CHUNK, CHUNK), CHUNK)

    load_gu.wait()
    load_dn.wait()
    with jax.named_scope("expert0"):

        def first_quarter(i, carry):
            acc[arow(i), :] = expert(0, i)[1]
            return carry

        lax.fori_loop(0, PEERS * SLOTS // CHUNK, first_quarter, 0)
    forward(1)
    forward(2)
    with jax.named_scope("expert12"):

        def middle(n, carry):
            k, i = 1 + n // 4, n % 4
            acc[arow(i), :] += expert(k, i)[1]
            return carry

        lax.fori_loop(0, 2 * PEERS * SLOTS // CHUNK, middle, 0)
    for c in range(3):
        for side in range(2):
            lo = side * (FFS // 2)
            fwd_copy(c, side).wait_recv()

    def ret_copy(j):
        return remote(
            rsend.at[j],
            rrecv.at[mine],
            ret_s.at[j],
            ret_r.at[mine],
            tok=mx * 2 + j // N_BLK,
            blk=j % N_BLK,
        )

    ret_own = pltpu.make_async_copy(rsend.at[mine], rrecv.at[mine], local.at[7])
    per = CHUNK // SLOTS
    with jax.named_scope("expert3"):

        def last(n, carry):
            i = (n + mine // per) % (PEERS // per)
            first, value = expert(3, i)
            rsend[pl.ds(first, per)] = (
                (acc[arow(i), :] + value).astype(BF16).reshape(per, SLOTS, D)
            )

            def start_ret(q, inner):
                j = i * per + (q + mine) % per

                @pl.when(j == mine)
                def _():
                    ret_own.start()

                @pl.when(j != mine)
                def _():
                    ret_copy(j).start()

                return inner

            return lax.fori_loop(0, per, start_ret, carry)

        lax.fori_loop(0, PEERS // per, last, 0)

    ret_own.wait()

    def wait_ret(d, carry):
        j = (mine + d) % PEERS
        remote(rsend.at[j], rrecv.at[j], ret_s.at[j], ret_r.at[j], tok=mx * 2 + 1 - mz).wait_recv()
        return carry

    lax.fori_loop(1, PEERS, wait_ret, 0)

    with jax.named_scope("combine"):
        back = [rrecv[z * N_BLK : (z + 1) * N_BLK].reshape(N_BLK * SLOTS, D) for z in range(2)]
        total = resid[...]
        for place, gate in ((place0, gate_cols[0]), (place1, gate_cols[1])):
            picked = lax.dot_general(
                place[...], back[0], TN, preferred_element_type=F32
            ) + lax.dot_general(place[...], back[1], TN, preferred_element_type=F32)
            total = total + gate * picked
        out[...] = total.astype(BF16)

    keep_cache.wait()
    for d in range(1, N_TOK):
        qkv_copy(d).wait_send()
        for r in range(REQ):
            cache_copy(r, d).wait_send()
            att_copy(r, d).wait_send()
    for c in range(3):
        for side in range(2):
            own_copy(c, side).wait_send()
            fwd_copy(c, side).wait_send()

    def drain(d, carry):
        disp_copy(d).wait_send()
        ret_copy((mine + d) % PEERS).wait_send()
        return carry

    lax.fori_loop(1, PEERS, drain, 0)


def cache_kernel(blocks, old, fresh, out, zeros, sems):
    zeros[...] = jnp.zeros_like(zeros)
    for r in range(REQ):
        count = blocks[r]
        pltpu.make_async_copy(
            fresh.at[r],
            out.at[r, pl.ds(pl.multiple_of(count * LANES, LANES), NEW)],
            sems.at[r, 12],
        ).start()
        for j in range(12):

            @pl.when(j < count)
            def _():
                pltpu.make_async_copy(
                    old.at[r, pl.ds(j * LANES, LANES)],
                    out.at[r, pl.ds(j * LANES, LANES)],
                    sems.at[r, j],
                ).start()

            @pl.when(j >= count)
            def _():
                pltpu.make_async_copy(
                    zeros, out.at[r, pl.ds((j + 4) * LANES, LANES)], sems.at[r, j]
                ).start()

    for r in range(REQ):
        pltpu.make_async_copy(fresh.at[r], out.at[r, pl.ds(0, NEW)], sems.at[r, 12]).wait()
        for j in range(12):
            pltpu.make_async_copy(zeros, out.at[r, pl.ds(0, LANES)], sems.at[r, j]).wait()


def body(
    states,
    gain_attn,
    w_qkv,
    w_out,
    cache_prev,
    cached_blocks,
    gain_moe,
    w_router,
    routes,
    w_gate_up,
    w_down,
):
    gains = jnp.stack([gain_attn, gain_moe]).astype(F32)
    routes_rows = jnp.transpose(routes[0], (2, 0, 1)).reshape(2, TOK)
    w_gu = jnp.transpose(w_gate_up[0], (0, 2, 1)).reshape(2 * FFS, D)
    vmem = pl.BlockSpec(memory_space=pltpu.VMEM)
    hbm = pl.BlockSpec(memory_space=pl.ANY)
    smem = pl.BlockSpec(memory_space=pltpu.SMEM)
    sem = pltpu.SemaphoreType.DMA
    out, cache_out, kv_new = pl.pallas_call(
        layer_kernel,
        name="layer",
        out_shape=(
            jax.ShapeDtypeStruct((TOK, D), BF16),
            jax.ShapeDtypeStruct((REQ, N_TOK, PART, 2, LANES), BF16),
            jax.ShapeDtypeStruct((REQ * NEW * 2, LANES), BF16),
        ),
        in_specs=[smem, vmem, vmem, vmem, vmem, hbm, hbm, hbm, hbm, hbm],
        out_specs=(vmem, hbm, vmem),
        scratch_shapes=[
            pltpu.VMEM((D, 3 * D), BF16),
            pltpu.VMEM((D, D), BF16),
            pltpu.VMEM((REQ, N_TOK, PART, 2, LANES), BF16),
            pltpu.VMEM((N_TOK, 3 * REQ, PER, LANES), BF16),
            pltpu.VMEM((3 * REQ, N_TOK, PER, LANES), BF16),
            pltpu.VMEM((CACHE + NEW, LANES), BF16),
            pltpu.VMEM((CACHE + NEW, LANES), BF16),
            pltpu.VMEM((2 * PART, LANES), F32),
            pltpu.VMEM((N_TOK, REQ, PER, LANES), BF16),
            pltpu.VMEM((TOK, D), BF16),
            pltpu.VMEM((TOK, D), F32),
            pltpu.VMEM((N_BLK * SLOTS, TOK), BF16),
            pltpu.VMEM((N_BLK * SLOTS, TOK), BF16),
            pltpu.VMEM((N_BLK, SLOTS, D), BF16),
            pltpu.VMEM((PEERS, SLOTS, D), BF16),
            pltpu.VMEM((4, 2 * FFS, D), BF16),
            pltpu.VMEM((4, FFS, D), BF16),
            pltpu.VMEM((PEERS * SLOTS, D), F32),
            pltpu.VMEM((PEERS, SLOTS, D), BF16),
            pltpu.VMEM((PEERS, SLOTS, D), BF16),
            sem((8,)),
            sem((REQ, N_TOK)),
            sem((REQ, N_TOK)),
            sem((REQ,)),
            sem((N_TOK,)),
            sem((N_TOK,)),
            sem((REQ, N_TOK)),
            sem((REQ, N_TOK)),
            sem((REQ,)),
            sem((3, 2)),
            sem((3, 2)),
            sem((3, 2)),
            sem((3, 2)),
            sem((PEERS,)),
            sem((PEERS,)),
            sem((PEERS,)),
            sem((PEERS,)),
        ],
        compiler_params=pltpu.CompilerParams(
            collective_id=0, has_side_effects=True, vmem_limit_bytes=60 * 1024 * 1024
        ),
    )(
        cached_blocks,
        states.reshape(TOK, D),
        gains,
        routes_rows,
        jnp.transpose(w_router),
        w_qkv,
        w_out,
        cache_prev,
        w_gu,
        w_down[0],
    )
    decode_cache = pl.pallas_call(
        cache_kernel,
        name="place_cache",
        out_shape=jax.ShapeDtypeStruct((REQ, CACHE + NEW, 2, LANES), BF16),
        in_specs=[smem, vmem, vmem],
        out_specs=hbm,
        scratch_shapes=[pltpu.VMEM((LANES, 2, LANES), BF16), sem((REQ, 13))],
    )(
        cached_blocks,
        cache_out.reshape(REQ, CACHE, 2, LANES),
        kv_new.reshape(REQ, NEW, 2, LANES),
    )
    return (out.reshape(REQ, PER, D), decode_cache)


def solution(mesh):
    return jax.shard_map(
        body,
        mesh=mesh,
        in_specs=(
            P("blk", "tok", None),
            P(),
            P(),
            P(),
            P("blk", "tok", None, None),
            P("blk"),
            P(),
            P(),
            P("tok", "blk", None, None),
            P("blk", None, None, "tok"),
            P("blk", "tok", None),
        ),
        out_specs=(P("blk", "tok", None), P("blk", None, None, "tok")),
        check_vma=False,
    )
```

time: 477 us -> 174 us (0.36)
  waiting for transfers between devices: 195 us -> 0 us
  Pallas kernels: 0 us -> 169 us
  local copies, waits for them, and re-layouts: 135 us -> 3.47 us
  matrix products: 58.2 us -> 0 us
  starting transfers between devices: 41.1 us -> 0 us
  other arithmetic: 30.9 us -> 0.61 us
  between operations: 14.3 us -> 0.66 us
    pallas_call x0 -> x2, Pallas kernels: none -> 169 us  [the longest x1 165 us: body(): pl.pallas_call(layer_kernel, name='layer', out_shape=(jax.ShapeDtypeStruc...]
    all_gather x2 -> x0, waiting for transfers between devices: 140 us -> none  [the longest x1 81.3 us: body(): lax.all_gather(w_down, 'tok', axis=1, tiled=True)]
    all_to_all x5 -> x0, waiting for transfers between devices: 54.2 us -> none  [the longest x1 24 us: body(): lax.all_to_all(cache_split, 'tok', split_axis=3, concat_axis=1, tiled=True)]
    dot_general x8 -> x0, matrix products: 43 us -> none  [the longest x1 11.9 us: body(): jnp.einsum('rhqk,rkhd->rqhd', weights, value_all, preferred_element_type=...]
    all_to_all x5 -> x0, starting transfers between devices: 41 us -> none  [the longest x1 10.3 us: body(): lax.all_to_all(outgoing, 'blk', split_axis=0, concat_axis=0, tiled=True)]
    unnamed x31 -> x3, local copies, waits for them, and re-layouts: 40.1 us -> 0.75 us
    reshape x9 -> x1, local copies, waits for them, and re-layouts: 31.3 us -> 0.66 us  [body(): routes_rows = jnp.transpose(routes[0], (2, 0, 1)).reshape(2, TOK)]
    all_gather x1 -> x0, local copies, waits for them, and re-layouts: 28.8 us -> none  [body(): lax.all_gather(w_gate_up, 'tok', axis=3, tiled=True)]
  transfers between devices with their start and end apart: 7 -> 0, of which waited for: 5 -> 0; matrix products, arithmetic and copies ran while one was open for 43% -> 0% of each run, Pallas kernels for 0% -> 0%
where the time goes in v1:
time: 174 us
  Pallas kernels  169 us (97%)
  local copies, waits for them, and re-layouts  3.47 us (2%)
    pallas_call x1, Pallas kernels, body(): pl.pallas_call(layer_kernel, name='layer', out_shape=(jax.ShapeDtypeStruc...  165 us
    pallas_call x1, Pallas kernels, body(): pl.pallas_call(cache_kernel, name='place_cache', out_shape=jax.ShapeDtype...  3.88 us

profile of v1, /device:TPU:1, one launch (start us, length us, event | category | flops | bytes accessed | tf_op | source)
XLA Modules:
  0.0 173.8 jit_solution(7587905595634036266)
XLA Ops:
  0.6 0.7 stack.9
  1.3 0.7 stack.10
  2.0 0.6 maximum_convert_fusion.gains
  2.6 0.7 copy.14
  3.3 0.7 reshape.23.routes
  4.0 165.2 %layer.1 = (bf16[192,1024]{1,0:T(8,128)(2,1)}, bf16[3,8,192,2,128]{4,3,2,1,0:T(2,128)(2,1)}, bf16[3072,128]{1,0:T(8,128)(2,1)}) custom-call(s32[3]{0:T(128)} %blocks.3, bf16[192,1024]{1,0:T(8,128)(2,1)} %bitcast.18, f32[2,1024]{1,0:T(2,128)} %maximum_convert_fusion.gains, s32[2,192]{1,0:T(2,128)} %reshape.23.routes, bf16[16,1024]{1,0:T(8,128)(2,1)} %bitcast.20, ...), custom_call_target="tpu_custom_call" | custom-call | tf_op jit(solution)/shard_map/layer/pallas_call | solution.py:566
  169.2 0.0 copy-start
  169.2 3.9 %place_cache.1 = bf16[3,2048,2,128]{3,2,1,0:T(2,128)(2,1)} custom-call(s32[3]{0:T(128)} %blocks.3, bf16[3,1536,2,128]{3,2,1,0:T(2,128)(2,1)} %bitcast.14, bf16[3,512,2,128]{3,2,1,0:T(2,128)(2,1)} %bitcast.16), custom_call_target="tpu_custom_call" | custom-call | tf_op jit(solution)/shard_map/place_cache/pallas_call | solution.py:630
  173.0 0.0 copy-done
  173.1 0.7 copy.16
Async XLA Ops:
  169.2 3.9 %copy-start = (bf16[192,1024]{1,0:T(8,128)(2,1)S(1)}, bf16[192,1024]{1,0:T(8,128)(2,1)}, u32[]{:S(2)}) copy-start(bf16[192,1024]{1,0:T(8,128)(2,1)} %get-tuple-element.5) | copy-start | bytes 1179652

commit v2 on v1

--- a/solution.py
+++ b/solution.py
@@ -18,6 +18,15 @@
 PART = CACHE // N_TOK
 FFS = 352
 QROWS = 256
+TOK_ORDER = ((1, 1), (3, 0), (3, 1), (1, 0), (2, 1), (2, 0), (0, 1))
+PLANES = ((0, 0), (1, 0), (1, 1), (0, 1))
+EXP_ORDER = tuple(
+    (*PLANES[i], (1, 0, 3, 2)[(k + i) % 4], c)
+    for c in range(2)
+    for k in range(4)
+    for i in range(4)
+    if (*PLANES[i], (1, 0, 3, 2)[(k + i) % 4], c) != (0, 0, 0, 0)
+)
 CHUNK = 256
 LANES = 128
 
@@ -29,7 +38,8 @@
 def layer_kernel(
     blocks,
     states,
-    gains,
+    gain_a,
+    gain_m,
     routes,
     router,
     w_qkv,
@@ -60,6 +70,7 @@
     acc,
     rsend,
     rrecv,
+    hid,
     local,
     cache_s,
     cache_r,
@@ -84,6 +95,19 @@
     mine = mz * N_BLK + mb
     right = ((mx + 1) % N_X) * 2 + mz
     left = ((mx + N_X - 1) % N_X) * 2 + mz
+    far_z, my, core = mb // 8, (mb // 2) % 4, mb % 2
+
+    def peer(i, way):
+        dx, dz = TOK_ORDER[i]
+        return ((mx + way * dx + N_X) % N_X) * 2 + (mz + dz) % 2
+
+    def pair_of(i, way):
+        dz, dfar, dy, dc = EXP_ORDER[i]
+        y = (my + way * dy + 4) % 4
+        return {
+            "tok": mx * 2 + (mz + dz) % 2,
+            "blk": (((far_z + dfar) % 2) * 4 + y) * 2 + (core + dc) % 2,
+        }
 
     def remote(src, dst, ssem, rsem, **where):
         return pltpu.make_async_remote_copy(
@@ -99,32 +123,28 @@
         return pl.ds(pl.multiple_of(t * LANES, LANES), LANES)
 
     barrier = pltpu.get_barrier_semaphore()
-    for d in range(1, N_TOK):
+    for i in range(N_TOK - 1):
         pl.semaphore_signal(
-            barrier, inc=1, device_id={"tok": (me + d) % N_TOK}, device_id_type=MESH
-        )
-
-    def greet(d, carry):
-        j = (mine + d) % PEERS
-        pl.semaphore_signal(
-            barrier,
-            inc=1,
-            device_id={"tok": mx * 2 + j // N_BLK, "blk": j % N_BLK},
-            device_id_type=MESH,
-        )
-        return carry
-
-    lax.fori_loop(1, PEERS, greet, 0)
-
-    load_qkv = pltpu.make_async_copy(w_qkv, wqkv, local.at[0])
+            barrier, inc=1, device_id={"tok": peer(i, 1)}, device_id_type=MESH
+        )
+    for i in range(PEERS - 1):
+        pl.semaphore_signal(barrier, inc=1, device_id=pair_of(i, 1), device_id_type=MESH)
+
+    load_qkv = [
+        pltpu.make_async_copy(
+            w_qkv.at[pl.ds(q * 256, 256)], wqkv.at[pl.ds(q * 256, 256)], local.at[8 + q]
+        )
+        for q in range(4)
+    ]
     load_out = pltpu.make_async_copy(w_out, wout, local.at[1])
     load_gu = pltpu.make_async_copy(w_gu, wg.at[0], local.at[2])
     load_dn = pltpu.make_async_copy(w_dn, wd.at[0], local.at[3])
-    load_qkv.start()
+    for part in load_qkv:
+        part.start()
     pl.semaphore_wait(barrier, N_TOK - 1 + PEERS - 1)
 
     def cache_copy(r, d):
-        t = (me + d) % N_TOK
+        t = peer(d - 1, 1)
         return remote(
             cache.at[r, :, :, lanes(t)],
             cbuf.at[r, me],
@@ -142,14 +162,16 @@
             cache_copy(r, d).start()
 
     send_cache(0)
+    send_cache(1)
     load_out.start()
     load_gu.start()
     load_dn.start()
 
     with jax.named_scope("project"):
         flat = states[...].astype(F32)
-        normed = normed_of(flat, gains[0:1, :]).astype(BF16)
-        load_qkv.wait()
+        normed = normed_of(flat, gain_a[...].astype(F32).reshape(1, D)).astype(BF16)
+        for part in load_qkv:
+            part.wait()
         for c in range(12):
             part = jnp.dot(
                 normed, wqkv[:, c * 256 : (c + 1) * 256], preferred_element_type=F32
@@ -161,14 +183,13 @@
                 ].reshape(REQ, PER, LANES)
 
     def qkv_copy(d):
-        t = (me + d) % N_TOK
+        t = peer(d - 1, 1)
         return remote(qs.at[t], qr.at[:, me], qkv_s.at[d], qkv_r.at[d], tok=t)
 
     qkv_own = pltpu.make_async_copy(qs.at[me], qr.at[:, me], local.at[4])
     qkv_own.start()
     for d in range(1, N_TOK):
         qkv_copy(d).start()
-    send_cache(1)
     send_cache(2)
 
     def chunk_of(ref_g, ref_d, c, lo, rows):
@@ -207,7 +228,8 @@
     send_own(0)
 
     with jax.named_scope("places"):
-        r0, r1 = routes[0:1, :], routes[1:2, :]
+        picks = jnp.concatenate([routes[r] for r in range(REQ)], axis=1)
+        r0, r1 = picks[0:1, :], picks[1:2, :]
         expert = lax.broadcasted_iota(jnp.int32, (N_BLK, TOK), 0)
         hot0 = (expert == r0).astype(F32)
         hot1 = (expert == r1).astype(F32)
@@ -226,13 +248,13 @@
 
     qkv_own.wait()
     for d in range(1, N_TOK):
-        s = (me + N_TOK - d) % N_TOK
+        s = peer(d - 1, -1)
         remote(qs.at[s], qr.at[:, s], qkv_s.at[d], qkv_r.at[d], tok=s).wait_recv()
 
     low_head = lax.broadcasted_iota(jnp.int32, (QROWS, LANES), 1) < LANES // 2
 
     def att_copy(r, d):
-        t = (me + d) % N_TOK
+        t = peer(d - 1, 1)
         return remote(
             asend.at[t, r],
             arecv.at[pl.ds(pl.multiple_of(r * PER, PER), PER), lanes(me)],
@@ -251,7 +273,7 @@
     def one_request(r, carry):
         cache_own(r).wait()
         for d in range(1, N_TOK):
-            s = (me + N_TOK - d) % N_TOK
+            s = peer(d - 1, -1)
             remote(
                 cache.at[r, :, :, lanes(s)], cbuf.at[r, s], cache_s.at[r, d], cache_r.at[r, d], tok=s
             ).wait_recv()
@@ -323,7 +345,7 @@
     for r in range(REQ):
         att_own(r).wait()
         for d in range(1, N_TOK):
-            s = (me + N_TOK - d) % N_TOK
+            s = peer(d - 1, -1)
             remote(
                 asend.at[s, r],
                 arecv.at[pl.ds(r * PER, PER), lanes(s)],
@@ -337,7 +359,7 @@
         resid[...] = states[...].astype(F32) + jnp.dot(
             arecv[...], wout[...], preferred_element_type=F32
         )
-        moe_in = normed_of(resid[...], gains[1:2, :]).astype(BF16)
+        moe_in = normed_of(resid[...], gain_m[...].astype(F32).reshape(1, D)).astype(BF16)
         both_places = (place0[...].astype(F32) + place1[...].astype(F32)).astype(BF16)
         dsend[...] = (
             jnp.dot(both_places, moe_in, preferred_element_type=F32)
@@ -345,26 +367,14 @@
             .reshape(N_BLK, SLOTS, D)
         )
 
-    def disp_copy(d):
-        j = (mine + d) % PEERS
-        e = j % N_BLK
-        return remote(
-            dsend.at[e],
-            drecv.at[mine],
-            disp_s.at[d],
-            disp_r.at[d],
-            tok=mx * 2 + j // N_BLK,
-            blk=e,
-        )
-
-    disp_own = pltpu.make_async_copy(dsend.at[mb], drecv.at[mine], local.at[6])
+    def disp_copy(i):
+        to = pair_of(i, 1)
+        return remote(dsend.at[to["blk"]], drecv.at[i], disp_s.at[i], disp_r.at[i], **to)
+
+    disp_own = pltpu.make_async_copy(dsend.at[mb], drecv.at[PEERS - 1], local.at[6])
+    for i in range(PEERS - 1):
+        disp_copy(i).start()
     disp_own.start()
-
-    def start_disp(d, carry):
-        disp_copy(d).start()
-        return carry
-
-    lax.fori_loop(1, PEERS, start_disp, 0)
     forward(0)
 
     with jax.named_scope("gates"):
@@ -390,24 +400,20 @@
 
         lax.fori_loop(0, REQ * 4, pair, 0)
 
+    forward(1)
     disp_own.wait()
-
-    def wait_disp(d, carry):
-        j = (mine + PEERS - d) % PEERS
-        remote(
-            dsend.at[j % N_BLK], drecv.at[j], disp_s.at[d], disp_r.at[d], tok=mx * 2 + 1 - mz
-        ).wait_recv()
-        return carry
-
-    lax.fori_loop(1, PEERS, wait_disp, 0)
-
-    def expert(k, i):
+    for i in range(PEERS - 1):
+        disp_copy(i).wait_recv()
+
+    def hidden_of(k, i):
         first = pl.multiple_of(i * (CHUNK // SLOTS), CHUNK // SLOTS)
         rows = drecv[pl.ds(first, CHUNK // SLOTS)].reshape(CHUNK, D)
         gate = lax.dot_general(rows, wg[k, :FFS, :], NT, preferred_element_type=F32)
         up = lax.dot_general(rows, wg[k, FFS:, :], NT, preferred_element_type=F32)
-        hidden = (jax.nn.gelu(gate, approximate=True) * up).astype(BF16)
-        return first, jnp.dot(hidden, wd[k], preferred_element_type=F32)
+        return (jax.nn.gelu(gate, approximate=True) * up).astype(BF16)
+
+    def expert(k, i):
+        return jnp.dot(hidden_of(k, i), wd[k], preferred_element_type=F32)
 
     def arow(i):
         return pl.ds(pl.multiple_of(i * CHUNK, CHUNK), CHUNK)
@@ -417,71 +423,60 @@
     with jax.named_scope("expert0"):
 
         def first_quarter(i, carry):
-            acc[arow(i), :] = expert(0, i)[1]
+            acc[arow(i), :] = expert(0, i)
             return carry
 
         lax.fori_loop(0, PEERS * SLOTS // CHUNK, first_quarter, 0)
-    forward(1)
     forward(2)
     with jax.named_scope("expert12"):
 
         def middle(n, carry):
             k, i = 1 + n // 4, n % 4
-            acc[arow(i), :] += expert(k, i)[1]
+            acc[arow(i), :] += expert(k, i)
             return carry
 
         lax.fori_loop(0, 2 * PEERS * SLOTS // CHUNK, middle, 0)
-    for c in range(3):
+    for c in range(2):
         for side in range(2):
-            lo = side * (FFS // 2)
             fwd_copy(c, side).wait_recv()
-
-    def ret_copy(j):
+    with jax.named_scope("hidden3"):
+
+        def last_hidden(i, carry):
+            hid[arow(i), :] = hidden_of(3, i)
+            return carry
+
+        lax.fori_loop(0, PEERS * SLOTS // CHUNK, last_hidden, 0)
+    for side in range(2):
+        fwd_copy(2, side).wait_recv()
+
+    def ret_copy(i):
         return remote(
-            rsend.at[j],
-            rrecv.at[mine],
-            ret_s.at[j],
-            ret_r.at[mine],
-            tok=mx * 2 + j // N_BLK,
-            blk=j % N_BLK,
-        )
-
-    ret_own = pltpu.make_async_copy(rsend.at[mine], rrecv.at[mine], local.at[7])
+            rsend.at[i], rrecv.at[mine], ret_s.at[i], ret_r.at[i], **pair_of(i, -1)
+        )
+
+    ret_own = pltpu.make_async_copy(rsend.at[PEERS - 1], rrecv.at[mine], local.at[7])
     per = CHUNK // SLOTS
     with jax.named_scope("expert3"):
-
-        def last(n, carry):
-            i = (n + mine // per) % (PEERS // per)
-            first, value = expert(3, i)
-            rsend[pl.ds(first, per)] = (
-                (acc[arow(i), :] + value).astype(BF16).reshape(per, SLOTS, D)
-            )
-
-            def start_ret(q, inner):
-                j = i * per + (q + mine) % per
-
-                @pl.when(j == mine)
-                def _():
+        for n in range(PEERS // per):
+            here = slice(n * CHUNK, (n + 1) * CHUNK)
+            value = acc[here, :] + jnp.dot(hid[here, :], wd[3], preferred_element_type=F32)
+            rsend[n * per : (n + 1) * per] = value.astype(BF16).reshape(per, SLOTS, D)
+            for i in range(n * per, (n + 1) * per):
+                if i == PEERS - 1:
                     ret_own.start()
-
-                @pl.when(j != mine)
-                def _():
-                    ret_copy(j).start()
-
-                return inner
-
-            return lax.fori_loop(0, per, start_ret, carry)
-
-        lax.fori_loop(0, PEERS // per, last, 0)
+                else:
+                    ret_copy(i).start()
 
     ret_own.wait()
-
-    def wait_ret(d, carry):
-        j = (mine + d) % PEERS
-        remote(rsend.at[j], rrecv.at[j], ret_s.at[j], ret_r.at[j], tok=mx * 2 + 1 - mz).wait_recv()
-        return carry
-
-    lax.fori_loop(1, PEERS, wait_ret, 0)
+    for i in range(PEERS - 1):
+        at = pair_of(i, 1)
+        remote(
+            rsend.at[i],
+            rrecv.at[((mz + EXP_ORDER[i][0]) % 2) * N_BLK + at["blk"]],
+            ret_s.at[i],
+            ret_r.at[i],
+            **at,
+        ).wait_recv()
 
     with jax.named_scope("combine"):
         back = [rrecv[z * N_BLK : (z + 1) * N_BLK].reshape(N_BLK * SLOTS, D) for z in range(2)]
@@ -504,32 +499,26 @@
             own_copy(c, side).wait_send()
             fwd_copy(c, side).wait_send()
 
-    def drain(d, carry):
-        disp_copy(d).wait_send()
-        ret_copy((mine + d) % PEERS).wait_send()
-        return carry
-
-    lax.fori_loop(1, PEERS, drain, 0)
-
-
-def cache_kernel(blocks, old, fresh, out, zeros, sems):
+    for i in range(PEERS - 1):
+        disp_copy(i).wait_send()
+        ret_copy(i).wait_send()
+
+
+def cache_kernel(blocks, old, fresh, out, old_v, fresh_v, zeros, load, sems):
+    loads = [
+        (
+            pltpu.make_async_copy(old.at[r], old_v.at[r], load.at[r, 0]),
+            pltpu.make_async_copy(fresh.at[r], fresh_v.at[r], load.at[r, 1]),
+        )
+        for r in range(REQ)
+    ]
+    for pair in loads:
+        for copy in pair:
+            copy.start()
     zeros[...] = jnp.zeros_like(zeros)
     for r in range(REQ):
         count = blocks[r]
-        pltpu.make_async_copy(
-            fresh.at[r],
-            out.at[r, pl.ds(pl.multiple_of(count * LANES, LANES), NEW)],
-            sems.at[r, 12],
-        ).start()
         for j in range(12):
-
-            @pl.when(j < count)
-            def _():
-                pltpu.make_async_copy(
-                    old.at[r, pl.ds(j * LANES, LANES)],
-                    out.at[r, pl.ds(j * LANES, LANES)],
-                    sems.at[r, j],
-                ).start()
 
             @pl.when(j >= count)
             def _():
@@ -538,7 +527,26 @@
                 ).start()
 
     for r in range(REQ):
-        pltpu.make_async_copy(fresh.at[r], out.at[r, pl.ds(0, NEW)], sems.at[r, 12]).wait()
+        count = blocks[r]
+        for copy in loads[r]:
+            copy.wait()
+        pltpu.make_async_copy(
+            fresh_v.at[r],
+            out.at[r, pl.ds(pl.multiple_of(count * LANES, LANES), NEW)],
+            sems.at[r, 12],
+        ).start()
+        for j in range(12):
+
+            @pl.when(j < count)
+            def _():
+                pltpu.make_async_copy(
+                    old_v.at[r, pl.ds(j * LANES, LANES)],
+                    out.at[r, pl.ds(j * LANES, LANES)],
+                    sems.at[r, j],
+                ).start()
+
+    for r in range(REQ):
+        pltpu.make_async_copy(fresh_v.at[r], out.at[r, pl.ds(0, NEW)], sems.at[r, 12]).wait()
         for j in range(12):
             pltpu.make_async_copy(zeros, out.at[r, pl.ds(0, LANES)], sems.at[r, j]).wait()
 
@@ -556,8 +564,7 @@
     w_gate_up,
     w_down,
 ):
-    gains = jnp.stack([gain_attn, gain_moe]).astype(F32)
-    routes_rows = jnp.transpose(routes[0], (2, 0, 1)).reshape(2, TOK)
+    routes_rows = jnp.transpose(routes[0], (0, 2, 1))
     w_gu = jnp.transpose(w_gate_up[0], (0, 2, 1)).reshape(2 * FFS, D)
     vmem = pl.BlockSpec(memory_space=pltpu.VMEM)
     hbm = pl.BlockSpec(memory_space=pl.ANY)
@@ -571,7 +578,7 @@
             jax.ShapeDtypeStruct((REQ, N_TOK, PART, 2, LANES), BF16),
             jax.ShapeDtypeStruct((REQ * NEW * 2, LANES), BF16),
         ),
-        in_specs=[smem, vmem, vmem, vmem, vmem, hbm, hbm, hbm, hbm, hbm],
+        in_specs=[smem, vmem, vmem, vmem, vmem, vmem, hbm, hbm, hbm, hbm, hbm],
         out_specs=(vmem, hbm, vmem),
         scratch_shapes=[
             pltpu.VMEM((D, 3 * D), BF16),
@@ -594,7 +601,8 @@
             pltpu.VMEM((PEERS * SLOTS, D), F32),
             pltpu.VMEM((PEERS, SLOTS, D), BF16),
             pltpu.VMEM((PEERS, SLOTS, D), BF16),
-            sem((8,)),
+            pltpu.VMEM((PEERS * SLOTS, FFS), BF16),
+            sem((12,)),
             sem((REQ, N_TOK)),
             sem((REQ, N_TOK)),
             sem((REQ,)),
@@ -618,7 +626,8 @@
     )(
         cached_blocks,
         states.reshape(TOK, D),
-        gains,
+        gain_attn,
+        gain_moe,
         routes_rows,
         jnp.transpose(w_router),
         w_qkv,
@@ -631,9 +640,15 @@
         cache_kernel,
         name="place_cache",
         out_shape=jax.ShapeDtypeStruct((REQ, CACHE + NEW, 2, LANES), BF16),
-        in_specs=[smem, vmem, vmem],
+        in_specs=[smem, hbm, hbm],
         out_specs=hbm,
-        scratch_shapes=[pltpu.VMEM((LANES, 2, LANES), BF16), sem((REQ, 13))],
+        scratch_shapes=[
+            pltpu.VMEM((REQ, CACHE, 2, LANES), BF16),
+            pltpu.VMEM((REQ, NEW, 2, LANES), BF16),
+            pltpu.VMEM((LANES, 2, LANES), BF16),
+            sem((REQ, 2)),
+            sem((REQ, 13)),
+        ],
     )(
         cached_blocks,
         cache_out.reshape(REQ, CACHE, 2, LANES),

time: 174 us -> 161 us (0.925)
  Pallas kernels: 169 us -> 159 us
  local copies, waits for them, and re-layouts: 3.47 us -> 0.75 us
    pallas_call x1, Pallas kernels: 165 us -> 155 us  [body(): pl.pallas_call(layer_kernel, name='layer', out_shape=(jax.ShapeDtypeStruc...]
where the time goes in v2:
time: 161 us
  Pallas kernels  159 us (99%)
    pallas_call x1, Pallas kernels, body(): pl.pallas_call(layer_kernel, name='layer', out_shape=(jax.ShapeDtypeStruc...  155 us
    pallas_call x1, Pallas kernels, body(): pl.pallas_call(cache_kernel, name='place_cache', out_shape=jax.ShapeDtype...  4.19 us

profile of v2, /device:TPU:1, one launch (start us, length us, event | category | flops | bytes accessed | tf_op | source)
XLA Modules:
  0.0 160.6 jit_solution(13821805549157516725)
XLA Ops:
  0.6 155.0 %layer.1 = (bf16[192,1024]{1,0:T(8,128)(2,1)}, bf16[3,8,192,2,128]{4,3,2,1,0:T(2,128)(2,1)}, bf16[3072,128]{1,0:T(8,128)(2,1)}) custom-call(s32[3]{0:T(128)} %blocks.3, bf16[192,1024]{1,0:T(8,128)(2,1)} %bitcast.18, bf16[1024]{0:T(1024)(128)(2,1)} %gain_a.1, bf16[1024]{0:T(1024)(128)(2,1)} %gain_m.1, s32[3,2,64]{2,1,0:T(2,128)} %bitcast.21, ...), custom_call_target="tpu_custom_call" | custom-call | tf_op jit(solution)/shard_map/layer/pallas_call | solution.py:573
  155.7 0.0 copy-start
  155.7 4.2 %place_cache.1 = bf16[3,2048,2,128]{3,2,1,0:T(2,128)(2,1)} custom-call(s32[3]{0:T(128)} %blocks.3, bf16[3,1536,2,128]{3,2,1,0:T(2,128)(2,1)} %bitcast.14, bf16[3,512,2,128]{3,2,1,0:T(2,128)(2,1)} %bitcast.16), custom_call_target="tpu_custom_call" | custom-call | tf_op jit(solution)/shard_map/place_cache/pallas_call | solution.py:639
  159.9 0.0 copy-done
  159.9 0.7 copy.14
Async XLA Ops:
  155.7 4.2 %copy-start = (bf16[192,1024]{1,0:T(8,128)(2,1)S(1)}, bf16[192,1024]{1,0:T(8,128)(2,1)}, u32[]{:S(2)}) copy-start(bf16[192,1024]{1,0:T(8,128)(2,1)} %get-tuple-element.5) | copy-start | bytes 1179652
